TPU v7x, 512 devices: a whole 4x4x16 slice. The times are simulated.
512 devices in a mesh: slab: 128 (over x, z, core), sub: 4 (over y).
Axes of the slice: x: 4, y: 4, z: 16, core: 2. Of those that a mesh axis runs over, the one named last changes fastest.
Arguments:
- ensemble: float32 [2, 15, 80, 65536], P(None, None, None, ('slab', 'sub')), may hold values from -6 to 6
- obs_value: float32 [2, 256], replicated, may hold values from -6 to 6
- obs_var: float32 [2, 256], replicated, may hold values from 0.5 to 4
- obs_owner: int32 [2, 256, 1], replicated, may hold values from 0 to 127; in each aligned block of 256 rows (0 to 255, 256 to 511, ..., all dimensions but the last counted through in order) at most 8 rows name the same one
- obs_column: int32 [2, 256], replicated, may hold values from 0 to 511
- home_block: int32 [2, 256], replicated, may hold values from -1 to 1
- batch_order: int32 [2], replicated, may hold values from 0 to 1, each once
Outputs:
- analysis: float32 [2, 15, 80, 65536], P(None, None, None, ('slab', 'sub'))
- assimilated_priors: float32 [2, 256, 160], replicated
Inputs may be any that keep to these rules, and one draw needn't show every extreme that they name: `obs_owner`: in each batch no slab owns more than 8 observations; in some batch one slab owns exactly 8. `batch_order`: each batch appears once.
All inputs are finite; a program needn't handle non-finite values.
Results may differ from a plain program's by a relative error of at most 0.00012.
Values sent between devices are 32-bit elements; how exact they have to be, the bound alone decides.
A program may use at most 64 MiB of HBM per device.

v0:
```python
import jax
import jax.numpy as jnp
from jax import lax
from jax.sharding import PartitionSpec as P

BANDS = 2
BLK = 16
BATCHES = 2
CAP = 8
HIGHEST = lax.Precision.HIGHEST


def gc_weight(first, second, nblocks, length):
    block_gap = jnp.abs(first - second)
    block_gap = jnp.minimum(block_gap, nblocks - block_gap)
    scaled_gap = block_gap.astype(jnp.float32) / length
    near_part = (
        ((-0.25 * scaled_gap + 0.5) * scaled_gap + 0.625) * scaled_gap**3
        - 5.0 / 3.0 * scaled_gap**2
        + 1.0
    )
    floored = jnp.maximum(scaled_gap, 1.0)
    far_part = (
        (
            (((scaled_gap / 12.0 - 0.5) * scaled_gap + 0.625) * scaled_gap + 5.0 / 3.0) * scaled_gap
            - 5.0
        )
        * scaled_gap
        + 4.0
        - 2.0 / (3.0 * floored)
    )
    return jnp.where(scaled_gap <= 1.0, near_part, jnp.where(scaled_gap < 2.0, far_part, 0.0))


def obs_statistics(current, values, variances, members):
    banded = current.reshape(current.shape[0], BANDS, members)
    whole_obs = jnp.sum(banded, axis=1)
    centre = jnp.mean(whole_obs, axis=1, keepdims=True)
    spread = jnp.sum((whole_obs - centre) ** 2, axis=1) / (members - 1) + 1e-06
    post_var = 1.0 / (1.0 / spread + 1.0 / variances)
    post_mean = post_var * (centre[:, 0] / spread + values / variances)
    increments = (post_mean - centre[:, 0])[:, None] + (jnp.sqrt(post_var / spread) - 1.0)[
        :, None
    ] * (whole_obs - centre)
    deviations = banded - jnp.mean(banded, axis=2, keepdims=True)
    return (deviations, spread, increments)


def update_pool(prior_pool, pool_homes, deviations, spread, increments, obs_homes, nblocks, decays):
    members = deviations.shape[2]
    banded = prior_pool.reshape(prior_pool.shape[0], prior_pool.shape[1], BANDS, members)
    new_bands = []
    for band_no in range(BANDS):
        pool_band = banded[:, :, band_no, :]
        pool_dev = pool_band - jnp.mean(pool_band, axis=2, keepdims=True)
        weights = (
            gc_weight(pool_homes[:, :, None], obs_homes[None, None, :], nblocks, decays[band_no])
            / ((members - 1) * spread)[None, None, :]
        )
        crossed = jnp.einsum("bpm,km->bpk", pool_dev, deviations[:, band_no, :], precision=HIGHEST)
        change = jnp.einsum("bpk,km->bpm", crossed * weights, increments, precision=HIGHEST)
        new_bands.append(pool_band + change)
    return jnp.stack(new_bands, axis=2).reshape(prior_pool.shape)


def update_state(ensemble, my_cols, deviations, spread, increments, obs_homes, nblocks, decays):
    members = ensemble.shape[2]
    new_bands = []
    for band_no in range(BANDS):
        band_layer = ensemble[band_no]
        layer_dev = band_layer - jnp.mean(band_layer, axis=1, keepdims=True)
        obs_dev = deviations[:, band_no, :]
        weights = (
            gc_weight((my_cols // BLK)[:, None], obs_homes[None, :], nblocks, decays[band_no])
            / ((members - 1) * spread)[None, :]
        )

        def one_level(level_dev):
            crossed = jnp.einsum("mc,km->ck", level_dev, obs_dev, precision=HIGHEST)
            return jnp.einsum("ck,km->mc", crossed * weights, increments, precision=HIGHEST)

        change = lax.map(one_level, layer_dev)
        new_bands.append(band_layer + change)
    return jnp.stack(new_bands, axis=0)


def slot_table(owners, slot_rank, slab_number, capacity):
    obs_count = owners.shape[1]
    matches = (owners == slab_number)[:, None, :] & (
        slot_rank[:, None, :] == jnp.arange(capacity, dtype=jnp.int32)[None, :, None]
    )
    slot_obs = jnp.sum(
        jnp.where(matches, jnp.arange(obs_count, dtype=jnp.int32)[None, None, :], 0), axis=2
    )
    slot_valid = jnp.any(matches, axis=2)
    return (slot_obs, slot_valid)


def per_device(ensemble, obs_value, obs_var, obs_owner, obs_column, home_block, batch_order):
    members = ensemble.shape[2]
    levels_count = ensemble.shape[1]
    cols_dev = ensemble.shape[3]
    slab_count = lax.axis_size("slab")
    sub_count = lax.axis_size("sub")
    slab_index = lax.axis_index("slab")
    sub_index = lax.axis_index("sub")
    obs_batch = obs_value.shape[1]
    capacity = CAP
    cols_slab = cols_dev * sub_count
    nblocks = cols_slab * slab_count // BLK
    span_broad = cols_slab // (4 * BLK)
    span_narrow = max(span_broad // 4, 1)
    decays = (float(span_broad), float(span_narrow))
    owners = obs_owner[:, :, 0]
    obs_home = jnp.mod((owners * cols_slab + obs_column) // BLK + home_block, nblocks)
    onehot = (owners[:, :, None] == jnp.arange(slab_count, dtype=jnp.int32)[None, None, :]).astype(
        jnp.int32
    )
    running = jnp.cumsum(onehot, axis=1) - 1
    slot_rank = jnp.sum(onehot * running, axis=2)
    slot_global = owners * capacity + slot_rank
    slot_obs, slot_valid = slot_table(owners, slot_rank, slab_index, capacity)
    slot_column = jnp.take_along_axis(obs_column, slot_obs, axis=1)
    slot_level = slot_obs % levels_count
    holder = slot_column // cols_dev
    local_col = slot_column % cols_dev
    picked = ensemble[:, slot_level, :, local_col]
    retain = slot_valid & (holder == sub_index)
    picked = jnp.where(retain[:, :, None, None], picked, 0.0).reshape(
        BATCHES, capacity, BANDS * members
    )
    slot_priors = lax.psum(picked, "sub")
    slot_homes = jnp.take_along_axis(obs_home, slot_obs, axis=1)
    my_cols = (slab_index * sub_count + sub_index) * cols_dev + jnp.arange(
        cols_dev, dtype=jnp.int32
    )
    recorded = jnp.zeros((BATCHES, obs_batch, BANDS * members), jnp.float32)
    for step_no in range(BATCHES):
        batch_id = batch_order[step_no]
        own_slots = slot_priors[batch_id]
        values = obs_value[batch_id]
        variances = obs_var[batch_id]
        obs_homes = obs_home[batch_id]
        gathered = lax.all_gather(own_slots, "slab", axis=0, tiled=True)
        current = gathered[slot_global[batch_id]]
        live = jnp.ones((obs_batch,), jnp.bool_)
        recorded = recorded.at[batch_id].set(current)
        deviations, spread, increments = obs_statistics(current, values, variances, members)
        increments = jnp.where(live[:, None], increments, 0.0)
        slot_priors = update_pool(
            slot_priors, slot_homes, deviations, spread, increments, obs_homes, nblocks, decays
        )
        ensemble = update_state(
            ensemble, my_cols, deviations, spread, increments, obs_homes, nblocks, decays
        )
    return (ensemble, recorded)


def solution(mesh):
    placed = (P(None, None, None, ("slab", "sub")), P(), P(), P(), P(), P(), P())
    return jax.shard_map(
        per_device,
        mesh=mesh,
        in_specs=placed,
        out_specs=(P(None, None, None, ("slab", "sub")), P()),
        check_vma=False,
    )
```

profile of v0, /device:TPU:1, one launch (start us, length us, event | category | flops | bytes accessed | tf_op | source)
XLA Modules:
  0.0 351.5 jit_solution(10229613459352276190)
XLA Ops:
  5.6 14.3 %psum.7 = f32[2,8,160]{2,1,0:T(8,128)S(1)} all-reduce(f32[2,8,160]{2,1,0:T(8,128)S(1)} %broadcast_select_fusion), channel_id=1, replica_groups=mesh['slab'=128,'sub'=4] {'sub'}, use_global_device_ids=true, to_apply=%region_6.8 | all-reduce | flops 2560 | bytes 20480 | tf_op jit(solution)/shard_map/psum | solution.py:132
  22.5 111.6 %all-gather = f32[1,1024,160]{2,1,0:T(8,128)S(1)} all-gather(f32[1,8,160]{2,1,0:T(8,128)S(1)} %constant_dynamic-slice_fusion.9), channel_id=2, replica_groups=mesh['slab'=128,'sub'=4] {'slab'}, dimensions={1}, use_global_device_ids=true | all-gather | bytes 660480 | tf_op jit(solution)/shard_map/all_gather | solution.py:144
  139.6 99.9 %all-gather.1 = f32[1,1024,160]{2,1,0:T(8,128)S(1)} all-gather(f32[1,8,160]{2,1,0:T(8,128)S(1)} %constant_dynamic-slice_fusion.4), channel_id=3, replica_groups=mesh['slab'=128,'sub'=4] {'slab'}, dimensions={1}, use_global_device_ids=true | all-gather | bytes 660480 | tf_op jit(solution)/shard_map/all_gather | solution.py:144
  245.5 24.5 %while.48 = (s32[]{:T(128)}, f32[15,80,128]{2,1,0:T(8,128)S(1)}, f32[15,80,128]{2,1,0:T(8,128)}, f32[256,80]{1,0:T(8,128)S(1)}, f32[256,80]{1,0:T(8,128)S(1)}, /...) while((s32[]{:T(128)}, f32[15,80,128]{2,1,0:T(8,128)S(1)}, ...), condition=%wide.region_24.26_spmd.clone, body=%wide.region_23.25_spmd.clone.sunk | while | flops 64094208 | bytes 560225 | solution.py:82
  270.8 26.6 %while.46 = (s32[]{:T(128)}, f32[15,80,128]{2,1,0:T(8,128)S(1)}, f32[15,80,128]{2,1,0:T(8,128)S(1)}, f32[256,80]{1,0:T(8,128)}, f32[256,80]{1,0:T(8,128)S(1)}, /...) while((s32[]{:T(128)}, f32[15,80,128]{2,1,0:T(8,128)S(1)}, ...), condition=%wide.region_12.14_spmd.clone, body=%wide.region_11.13_spmd.clone.sunk | while | flops 64094208 | bytes 559717 | solution.py:82
  270.8 1.4 convolution_multiply_fusion.10
  272.6 1.4 convolution_multiply_fusion.10
  274.4 1.4 convolution_multiply_fusion.10
  276.2 1.4 convolution_multiply_fusion.10
  277.9 1.4 convolution_multiply_fusion.10
  279.7 1.4 convolution_multiply_fusion.10
  281.5 1.4 convolution_multiply_fusion.10
  283.3 1.4 convolution_multiply_fusion.10
  285.0 1.4 convolution_multiply_fusion.10
  286.8 1.4 convolution_multiply_fusion.10
  288.6 1.4 convolution_multiply_fusion.10
  290.3 1.4 convolution_multiply_fusion.10
  292.1 1.4 convolution_multiply_fusion.10
  293.9 1.4 convolution_multiply_fusion.10
  295.7 1.4 convolution_multiply_fusion.10
  299.0 24.5 %while.49 = (s32[]{:T(128)}, f32[15,80,128]{2,1,0:T(8,128)S(1)}, f32[15,80,128]{2,1,0:T(8,128)}, f32[256,80]{1,0:T(8,128)S(1)}, f32[256,80]{1,0:T(8,128)S(1)}, /...) while((s32[]{:T(128)}, f32[15,80,128]{2,1,0:T(8,128)S(1)}, ...), condition=%wide.region_27.29_spmd.clone, body=%wide.region_26.28_spmd.clone.sunk | while | flops 64094208 | bytes 560225 | solution.py:82
  324.4 24.6 %while.47 = (s32[]{:T(128)}, f32[15,80,128]{2,1,0:T(8,128)S(1)}, f32[15,80,128]{2,1,0:T(8,128)}, f32[256,80]{1,0:T(8,128)S(1)}, f32[256,80]{1,0:T(8,128)S(1)}, /...) while((s32[]{:T(128)}, f32[15,80,128]{2,1,0:T(8,128)S(1)}, ...), condition=%wide.region_21.23_spmd.clone, body=%wide.region_20.22_spmd.clone.sunk | while | flops 64094208 | bytes 560225 | solution.py:82
  327.7 1.2 convolution_multiply_fusion.11
  349.0 1.3 add_bitcast_fusion.1
  (228 shorter events, 95.6 us)
Async XLA Ops:
  0.6 1.6 copy-start.3
  0.6 2.1 copy-start
  2.0 1.8 copy-start.1
  3.8 16.2 %copy-start.4 = (s32[2]{0:T(128)S(1)}, s32[2]{0:T(128)}, u32[]{:S(2)}) copy-start(s32[2]{0:T(128)} %param.27) | copy-start | bytes 28
  4.8 131.3 %copy-start.5 = (s32[2,256]{1,0:T(2,128)S(1)}, s32[2,256]{1,0:T(2,128)}, u32[]{:S(2)}) copy-start(s32[2,256]{1,0:T(2,128)} %param.26) | copy-start | bytes 6148
  136.2 1.3 copy-start.6
  136.2 1.3 copy-start.7
  137.5 2.0 copy-start.8
  137.8 101.7 %copy-start.10 = (s32[1,256]{1,0:T(1,128)}, s32[1,256]{1,0:T(1,128)S(1)}, u32[]{:S(2)}) copy-start(s32[1,256]{1,0:T(1,128)S(1)} %get-tuple-element.436) | copy-start | bytes 3076
  239.5 1.0 copy-start.12
  244.5 1.0 copy-start.9
  244.5 1.0 copy-start.11
  270.0 0.8 copy-start.13
  297.7 1.3 copy-start.14
  323.5 0.8 copy-start.2
where the time goes:
time: 355 us; the launch traced here: 352 us
  blocking collectives  226 us (64%)
  matrix products  99.2 us (28%)
  local copies, waits for them, and re-layouts  10.4 us (3%)
  other arithmetic  9.13 us (3%)
  between operations  5.16 us (1%)
    all_gather x2, blocking collectives, per_device(): gathered = lax.all_gather(own_slots, 'slab', axis=0, tiled=True)  212 us
    dot_general x60, matrix products, one_level(): crossed = jnp.einsum('mc,km->ck', level_dev, obs_dev, precision=HIGHEST)  76 us
    dot_general x60, matrix products, one_level(): jnp.einsum('ck,km->mc', crossed * weights, increments, precision=HIGHEST)  22.5 us
    psum x1, blocking collectives, per_device(): slot_priors = lax.psum(picked, 'sub')  14.3 us

commit v1 on v0

--- a/solution.py
+++ b/solution.py
@@ -141,7 +141,9 @@
         values = obs_value[batch_id]
         variances = obs_var[batch_id]
         obs_homes = obs_home[batch_id]
-        gathered = lax.all_gather(own_slots, "slab", axis=0, tiled=True)
+        gathered = jnp.concatenate(
+            lax.all_to_all(jnp.stack([own_slots] * lax.axis_size("slab")), "slab", 0, 0), axis=0
+        )
         current = gathered[slot_global[batch_id]]
         live = jnp.ones((obs_batch,), jnp.bool_)
         recorded = recorded.at[batch_id].set(current)

time: 355 us -> 230 us (0.65)
  blocking collectives: 226 us -> 14.3 us
  waiting for transfers between devices: 0 us -> 49.3 us
  starting transfers between devices: 0 us -> 32.3 us
  local copies, waits for them, and re-layouts: 10.4 us -> 14.7 us
    all_gather x2 -> x0, blocking collectives: 212 us -> none  [per_device(): gathered = lax.all_gather(own_slots, 'slab', axis=0, tiled=True)]
    all_to_all x0 -> x2, waiting for transfers between devices: none -> 49.3 us  [per_device(): lax.all_to_all(jnp.stack([own_slots] * lax.axis_size('slab')), 'slab', 0, 0)]
    all_to_all x0 -> x2, starting transfers between devices: none -> 32.3 us  [per_device(): lax.all_to_all(jnp.stack([own_slots] * lax.axis_size('slab')), 'slab', 0, 0)]
  transfers between devices with their start and end apart: 0 -> 2, of which waited for: 0 -> 1; matrix products, arithmetic and copies ran while one was open for 0% -> 25% of each run, Pallas kernels for 0% -> 0%
where the time goes in v1:
time: 230 us; the launch traced here: 226 us
  matrix products  99.1 us (43%)
  waiting for transfers between devices  49.3 us (21%)
  starting transfers between devices  32.3 us (14%)
  local copies, waits for them, and re-layouts  14.7 us (6%)
  blocking collectives  14.3 us (6%)
  other arithmetic  9.16 us (4%)
  between operations  5.08 us (2%)
    dot_general x60, matrix products, one_level(): crossed = jnp.einsum('mc,km->ck', level_dev, obs_dev, precision=HIGHEST)  75.8 us
    all_to_all x2, waiting for transfers between devices, per_device(): lax.all_to_all(jnp.stack([own_slots] * lax.axis_size('slab')), 'slab', 0, 0)  49.3 us
    all_to_all x2, starting transfers between devices, per_device(): lax.all_to_all(jnp.stack([own_slots] * lax.axis_size('slab')), 'slab', 0, 0)  32.3 us
    dot_general x60, matrix products, one_level(): jnp.einsum('ck,km->mc', crossed * weights, increments, precision=HIGHEST)  22.6 us
    psum x1, blocking collectives, per_device(): slot_priors = lax.psum(picked, 'sub')  14.3 us
    unnamed x31, local copies, waits for them, and re-layouts  4.95 us
  transfers between devices with their start and end apart: 2, of which 1 were waited for; matrix products, arithmetic and copies ran while one was open for 25% of the time, Pallas kernels for 0%

profile of v1, /device:TPU:1, one launch (start us, length us, event | category | flops | bytes accessed | tf_op | source)
XLA Modules:
  0.0 225.8 jit_solution(542486844694275009)
XLA Ops:
  6.3 14.3 %psum.7 = f32[2,8,160]{2,1,0:T(8,128)S(1)} all-reduce(f32[2,8,160]{2,1,0:T(8,128)S(1)} %broadcast_select_fusion), channel_id=1, replica_groups=mesh['slab'=128,'sub'=4] {'sub'}, use_global_device_ids=true, to_apply=%region_6.8 | all-reduce | flops 2560 | bytes 20480 | tf_op jit(solution)/shard_map/psum | solution.py:132
  24.2 23.3 %all-to-all-start = ((f32[128,8,160]{2,1,0:T(8,128)}), f32[128,8,160]{2,1,0:T(8,128)S(1)}, u32[]{:S(2)}, u32[]{:S(2)}) async-start(f32[128,8,160]{2,1,0:T(8,128)} %stack.24), calls=%async_computation | async-start | bytes 2097152 | tf_op jit(solution)/shard_map/all_to_all | solution.py:145
  52.6 49.3 %all-to-all-done = f32[128,8,160]{2,1,0:T(8,128)S(1)} async-done(((f32[128,8,160]{2,1,0:T(8,128)}), f32[128,8,160]{2,1,0:T(8,128)S(1)}, u32[]{:S(2)}, u32[]{:S(2)}) %all-to-all-start) | async-done | bytes 655392 | tf_op jit(solution)/shard_map/all_to_all | solution.py:145
  105.3 9.0 %all-to-all-start.1 = ((f32[128,8,160]{2,1,0:T(8,128)}), f32[128,8,160]{2,1,0:T(8,128)}, u32[]{:S(2)}, u32[]{:S(2)}) async-start(f32[128,8,160]{2,1,0:T(8,128)} %stack.28), calls=%async_computation.1 | async-start | bytes 2097152 | tf_op jit(solution)/shard_map/all_to_all | solution.py:145
  114.5 24.6 %while.48 = (s32[]{:T(128)}, f32[15,80,128]{2,1,0:T(8,128)S(1)}, f32[15,80,128]{2,1,0:T(8,128)}, f32[256,80]{1,0:T(8,128)S(1)}, f32[256,80]{1,0:T(8,128)S(1)}, /...) while((s32[]{:T(128)}, f32[15,80,128]{2,1,0:T(8,128)S(1)}, ...), condition=%wide.region_24.26_spmd.clone, body=%wide.region_23.25_spmd.clone.sunk | while | flops 64094208 | bytes 560225 | solution.py:82
  139.8 26.5 %while.46 = (s32[]{:T(128)}, f32[15,80,128]{2,1,0:T(8,128)S(1)}, f32[15,80,128]{2,1,0:T(8,128)S(1)}, f32[256,80]{1,0:T(8,128)}, f32[256,80]{1,0:T(8,128)S(1)}, /...) while((s32[]{:T(128)}, f32[15,80,128]{2,1,0:T(8,128)S(1)}, ...), condition=%wide.region_12.14_spmd.clone, body=%wide.region_11.13_spmd.clone.sunk | while | flops 64094208 | bytes 559717 | solution.py:82
  139.8 1.4 convolution_multiply_fusion.10
  141.6 1.4 convolution_multiply_fusion.10
  143.4 1.4 convolution_multiply_fusion.10
  145.1 1.4 convolution_multiply_fusion.10
  146.9 1.4 convolution_multiply_fusion.10
  148.7 1.4 convolution_multiply_fusion.10
  150.4 1.4 convolution_multiply_fusion.10
  152.2 1.4 convolution_multiply_fusion.10
  154.0 1.4 convolution_multiply_fusion.10
  155.7 1.4 convolution_multiply_fusion.10
  157.5 1.4 convolution_multiply_fusion.10
  159.2 1.4 convolution_multiply_fusion.10
  161.0 1.4 convolution_multiply_fusion.10
  162.8 1.4 convolution_multiply_fusion.10
  164.5 1.4 convolution_multiply_fusion.10
  168.8 2.2 gather_fusion.2
  173.2 24.5 %while.49 = (s32[]{:T(128)}, f32[15,80,128]{2,1,0:T(8,128)S(1)}, f32[15,80,128]{2,1,0:T(8,128)}, f32[256,80]{1,0:T(8,128)S(1)}, f32[256,80]{1,0:T(8,128)S(1)}, /...) while((s32[]{:T(128)}, f32[15,80,128]{2,1,0:T(8,128)S(1)}, ...), condition=%wide.region_27.29_spmd.clone, body=%wide.region_26.28_spmd.clone.sunk | while | flops 64094208 | bytes 560225 | solution.py:82
  198.6 24.6 %while.47 = (s32[]{:T(128)}, f32[15,80,128]{2,1,0:T(8,128)S(1)}, f32[15,80,128]{2,1,0:T(8,128)}, f32[256,80]{1,0:T(8,128)S(1)}, f32[256,80]{1,0:T(8,128)S(1)}, /...) while((s32[]{:T(128)}, f32[15,80,128]{2,1,0:T(8,128)S(1)}, ...), condition=%wide.region_21.23_spmd.clone, body=%wide.region_20.22_spmd.clone.sunk | while | flops 64094208 | bytes 560225 | solution.py:82
  (224 shorter events, 100.4 us)
Async XLA Ops:
  0.6 2.2 copy-start.3
  0.6 2.9 %copy-start = (s32[2,256]{1,0:T(2,128)S(1)}, s32[2,256]{1,0:T(2,128)}, u32[]{:S(2)}) copy-start(s32[2,256]{1,0:T(2,128)} %param.25) | copy-start | bytes 6148
  2.7 1.8 copy-start.1
  4.4 16.2 %copy-start.4 = (s32[2]{0:T(128)S(1)}, s32[2]{0:T(128)}, u32[]{:S(2)}) copy-start(s32[2]{0:T(128)} %param.27) | copy-start | bytes 28
  24.2 24.7 %copy-start.5 = (s32[2,256]{1,0:T(2,128)S(1)}, s32[2,256]{1,0:T(2,128)}, u32[]{:S(2)}) copy-start(s32[2,256]{1,0:T(2,128)} %param.26) | copy-start | bytes 6148
  24.2 26.5 %copy-start.6 = (f32[2,256]{1,0:T(2,128)S(1)}, f32[2,256]{1,0:T(2,128)}, u32[]{:S(2)}) copy-start(f32[2,256]{1,0:T(2,128)} %param.22) | copy-start | bytes 6148
  24.2 26.5 %copy-start.7 = (f32[2,256]{1,0:T(2,128)S(1)}, f32[2,256]{1,0:T(2,128)}, u32[]{:S(2)}) copy-start(f32[2,256]{1,0:T(2,128)} %param.23) | copy-start | bytes 6148
  24.2 26.5 %copy-start.8 = (s32[3]{0:T(128)S(1)}, s32[3]{0:T(128)}, u32[]{:S(2)}) copy-start(s32[3]{0:T(128)} %constant.293.clone.1) | copy-start | bytes 40
  24.2 77.7 %all-to-all-start = ((f32[128,8,160]{2,1,0:T(8,128)}), f32[128,8,160]{2,1,0:T(8,128)S(1)}, u32[]{:S(2)}, u32[]{:S(2)}) async-start(f32[128,8,160]{2,1,0:T(8,128)} %stack.24), calls=%async_computation | async-start | bytes 2097152 | tf_op jit(solution)/shard_map/all_to_all | solution.py:145
  105.3 63.4 %all-to-all-start.1 = ((f32[128,8,160]{2,1,0:T(8,128)}), f32[128,8,160]{2,1,0:T(8,128)}, u32[]{:S(2)}, u32[]{:S(2)}) async-start(f32[128,8,160]{2,1,0:T(8,128)} %stack.28), calls=%async_computation.1 | async-start | bytes 2097152 | tf_op jit(solution)/shard_map/all_to_all | solution.py:145
  166.3 0.5 copy-start.9
  172.6 0.6 copy-start.10
  197.8 0.8 copy-start.2
